TPU v7x, 512 devices: a whole 4x8x8 slice. The times are simulated.
512 devices in a mesh: dp: 128 (over y, x, z_lo, core), strip: 4 (over z_hi).
Axes of the slice: x: 4, y: 8, z: 8 (z_hi: 4, z_lo: 2; z = z_hi * 2 + z_lo), core: 2. Of those that a mesh axis runs over, the one named last changes fastest.
Arguments:
- latents: bfloat16 [128, 4, 320, 128], P('dp', 'strip'), may hold values from -6 to 6
- cotangent: bfloat16 [128, 4, 320, 128], P('dp', 'strip'), may hold values from -16 to 16
- weight: bfloat16 [320, 2880], P('strip'), may hold values from -0.109375 to 0.109375
- master: float32 [512, 2880], P('dp'), may hold values from -0.21875 to 0.21875
- first_moment: float32 [512, 2880], P('dp'), may hold values from -6 to 6
- second_moment: float32 [512, 2880], P('dp'), may hold values from 0.005 to 0.05
- owner_list: int32 [320], replicated, may hold values from 0 to 127, as said below
Outputs:
- output: bfloat16 [128, 4, 320, 128], P('dp', 'strip')
- grad_input: bfloat16 [128, 4, 320, 128], P('dp', 'strip')
- new_weight: bfloat16 [320, 2880], P('strip')
- new_master: float32 [512, 2880], P('dp')
- new_first: float32 [512, 2880], P('dp')
- new_second: float32 [512, 2880], P('dp')
Inputs may be any that keep to these rules, and one draw needn't show every extreme that they name: `owner_list`: each of the 128 ranks owns at least one and at most 4 buckets, and some rank owns exactly 4.
All inputs are finite; a program needn't handle non-finite values.
Results may differ from a plain program's by a relative error of at most 0.0033.
Values may be sent and summed in bfloat16 or wider, within the bound.
No kernel may reach another device: no remote copies, remote signals or barrier semaphores. Data moves between devices by JAX's collectives and lax.ppermute only.
A program may use at most 64 MiB of HBM per device.

v0:
```python
import jax
import jax.numpy as jnp
from jax import lax
from jax.sharding import PartitionSpec as P

beta_first = 0.9
beta_second = 0.999
learn_rate = 0.01
epsilon = 1e-08
bias_first = 1.0 - 0.9**10
bias_second = 1.0 - 0.999**10


def extended(cells, sides, width):
    for axis, dim in sides:
        count = lax.axis_size(axis)
        ends = count - 1
        head = lax.slice_in_dim(cells, 0, width, axis=dim)
        tail = lax.slice_in_dim(cells, cells.shape[dim] - width, cells.shape[dim], axis=dim)
        cells = jnp.concatenate(
            [
                lax.ppermute(tail, axis, [(i, (i + 1) % count) for i in range(ends)]),
                cells,
                lax.ppermute(head, axis, [((i + 1) % count, i) for i in range(ends)]),
            ],
            axis=dim,
        )
    return cells


def patches(padded, direction):
    widened = jnp.pad(padded, ((0, 0), (0, 0), (1, 1)))
    height = padded.shape[0] - 2
    across = padded.shape[2]
    pieces = []
    for row_step in (-1, 0, 1):
        for col_step in (-1, 0, 1):
            row_start = 1 + direction * row_step
            col_start = 1 + direction * col_step
            pieces.append(
                widened[row_start : row_start + height, :, col_start : col_start + across]
            )
    return jnp.concatenate(pieces, axis=1)


def flipped(weight):
    channels = weight.shape[0]
    return weight.reshape(channels, 9, channels).transpose(2, 1, 0).reshape(channels, 9 * channels)


def slot_tables(owner_list, capacity):
    count = owner_list.shape[0]
    same_owner = owner_list[:, None] == owner_list[None, :]
    earlier = (
        jnp.arange(count, dtype=jnp.int32)[None, :] < jnp.arange(count, dtype=jnp.int32)[:, None]
    )
    within = jnp.sum((same_owner & earlier).astype(jnp.int32), axis=1)
    return owner_list * capacity + within


def adam_update(grads, master, first_moment, second_moment, filled):
    first_new = beta_first * first_moment + (1.0 - beta_first) * grads
    second_new = beta_second * second_moment + (1.0 - beta_second) * grads * grads
    update = learn_rate * (first_new / bias_first) / (jnp.sqrt(second_new / bias_second) + epsilon)
    keep = filled[:, None]
    return (
        jnp.where(keep, master - update, master),
        jnp.where(keep, first_new, first_moment),
        jnp.where(keep, second_new, second_moment),
    )


def local(latents, cotangent, weight, master, first_moment, second_moment, owner_list):
    full_weight = lax.all_gather(weight, "strip", axis=0, tiled=True)
    channels = full_weight.shape[0]
    pixels = latents[0]
    upstream = cotangent[0]
    pixels_float = pixels.astype(jnp.float32)
    active = jax.nn.silu(pixels_float).astype(jnp.bfloat16)
    active_rim = extended(active, (("strip", 0),), 1)
    forward_cols = patches(active_rim, 1)
    convolved = jnp.einsum(
        "ok,hkw->how", full_weight, forward_cols, preferred_element_type=jnp.float32
    )
    output = (pixels_float + convolved).astype(jnp.bfloat16)
    upstream_rim = extended(upstream, (("strip", 0),), 1)
    backward_cols = patches(upstream_rim, -1)
    spread = jnp.einsum(
        "ck,hkw->hcw", flipped(full_weight), backward_cols, preferred_element_type=jnp.float32
    )
    sigmoid_val = jax.nn.sigmoid(pixels_float)
    derivative = sigmoid_val * (1.0 + pixels_float * (1.0 - sigmoid_val))
    grad_input = (upstream.astype(jnp.float32) + spread * derivative).astype(jnp.bfloat16)
    partial_grad = jnp.einsum(
        "how,hkw->ok", upstream, forward_cols, preferred_element_type=jnp.float32
    )
    capacity = master.shape[0]
    owners = lax.axis_size("dp")
    owner_rank = lax.axis_index("dp")
    slot_ids = slot_tables(owner_list, capacity)
    matches = slot_ids[None, :] == jnp.arange(owners * capacity, dtype=jnp.int32)[:, None]
    bucket = jnp.sum(jnp.where(matches, jnp.arange(channels, dtype=jnp.int32)[None, :], 0), axis=1)
    filled = jnp.any(matches, axis=1)
    source_row = jnp.where(filled, bucket, channels)
    my_filled = lax.dynamic_slice_in_dim(filled, owner_rank * capacity, capacity)
    outgoing = jnp.take(partial_grad, source_row, axis=0, mode="fill", fill_value=0.0).reshape(
        owners, capacity, 9 * channels
    )
    incoming = lax.all_to_all(
        outgoing.astype(jnp.bfloat16), "dp", split_axis=0, concat_axis=0, tiled=True
    ).astype(outgoing.dtype)
    owned_grad = lax.psum(jnp.sum(incoming, axis=0).astype(jnp.bfloat16), "strip").astype(
        jnp.float32
    )
    pixel_count = (
        latents.shape[0] * owners * pixels.shape[0] * lax.axis_size("strip") * pixels.shape[2]
    )
    gradient = owned_grad / jnp.sqrt(jnp.float32(pixel_count))
    new_master, new_first, new_second = adam_update(
        gradient, master, first_moment, second_moment, my_filled
    )
    published = lax.all_gather(new_master.astype(jnp.bfloat16), "dp", axis=0, tiled=True)
    quarter = weight.shape[0]
    wanted = lax.dynamic_slice_in_dim(slot_ids, lax.axis_index("strip") * quarter, quarter)
    new_weight = published[wanted]
    return (output[None], grad_input[None], new_weight, new_master, new_first, new_second)


def solution(mesh):
    in_specs = (
        P("dp", "strip", None, None),
        P("dp", "strip", None, None),
        P("strip", None),
        P("dp", None),
        P("dp", None),
        P("dp", None),
        P(),
    )
    out_specs = (
        P("dp", "strip", None, None),
        P("dp", "strip", None, None),
        P("strip", None),
        P("dp", None),
        P("dp", None),
        P("dp", None),
    )
    return jax.shard_map(local, mesh=mesh, in_specs=in_specs, out_specs=out_specs, check_vma=False)
```

profile of v0, /device:TPU:8, one launch (start us, length us, event | category | flops | bytes accessed | tf_op | source)
XLA Modules:
  0.0 371.5 jit_solution(15134228021462257407)
XLA Ops:
  7.2 0.9 fusion.17
  8.1 1.3 collective-permute-start.1
  9.4 6.7 %collective-permute-start = (bf16[1,320,128]{2,1,0:T(8,128)(2,1)S(1)}, bf16[1,320,128]{2,1,0:T(8,128)(2,1)S(1)}, u32[]{:S(2)}, u32[]{:S(2)}) collective-permute-start(bf16[1,320,128]{2,1,0:T(8,128)(2,1)S(1)} %fusion.17), channel_id=1, source_target_pairs={{0,1},{1,2},{2,3},{4,5},{5,6},{6,7},{8,9},{9,10},{10,11},{12,13},{... | collective-permute-start | bytes 245768 | tf_op jit(solution)/shard_map/ppermute | solution.py:22
  16.1 1.0 convert_reduce_fusion
  18.7 1.0 constant_dynamic-update-slice_fusion.1
  20.0 0.8 copy-done.1
  20.8 1.5 convolution_bitcast_fusion
  22.4 3.7 gather_fusion
  26.1 4.7 %gather.10 = bf16[128,4,2880]{2,1,0:T(4,128)(2,1)S(1)} reshape(bf16[512,2880]{1,0:T(8,128)(2,1)} %gather_fusion) | data formatting | bytes 5898240 | tf_op jit(solution)/shard_map/jit(_take)/gather | solution.py:106
  30.7 3.7 select_convert_fusion
  34.4 13.5 %all-to-all-start = ((bf16[128,4,2880]{2,1,0:T(4,128)(2,1)}), bf16[128,4,2880]{2,1,0:T(4,128)(2,1)S(1)}, u32[]{:S(2)}, u32[]{:S(2)}) async-start(bf16[128,4,2880]{2,1,0:T(4,128)(2,1)} %select_convert_fusion), calls=%async_computation | async-start | bytes 6029312 | tf_op jit(solution)/shard_map/all_to_all | solution.py:109
  48.9 69.2 %all-to-all-done = bf16[128,4,2880]{2,1,0:T(4,128)(2,1)S(1)} async-done(((bf16[128,4,2880]{2,1,0:T(4,128)(2,1)}), bf16[128,4,2880]{2,1,0:T(4,128)(2,1)S(1)}, u32[]{:S(2)}, u32[]{:S(2)}) %all-to-all-start) | async-done | bytes 2949152 | tf_op jit(solution)/shard_map/all_to_all | solution.py:109
  118.1 1.3 reduce_sum.32
  119.4 25.1 %psum.7 = bf16[4,2880]{1,0:T(4,128)(2,1)S(1)} all-reduce(bf16[4,2880]{1,0:T(4,128)(2,1)S(1)} %reduce_sum.32), channel_id=1, replica_groups=mesh['dp'=128,'strip'=4] {'strip'}, use_global_device_ids=true, to_apply=%region_4.5 | all-reduce | flops 11520 | bytes 46080 | tf_op jit(solution)/shard_map/psum | solution.py:112
  145.3 1.3 collective-permute-start.3
  146.6 5.6 %collective-permute-start.2 = (bf16[1,320,128]{2,1,0:T(8,128)(2,1)S(1)}, bf16[1,320,128]{2,1,0:T(8,128)(2,1)S(1)}, u32[]{:S(2)}, u32[]{:S(2)}) collective-permute-start(bf16[1,320,128]{2,1,0:T(8,128)(2,1)S(1)} %bitcast.62), channel_id=1, source_target_pairs={{0,1},{1,2},{2,3},{4,5},{5,6},{6,7},{8,9},{9,10},{10,11},{12,13},{... | collective-permute-start | bytes 245768 | tf_op jit(solution)/shard_map/ppermute | solution.py:22
  152.6 1.6 collective-permute-done.2
  160.4 3.3 copy.17
  163.7 2.5 copy.18
  166.2 3.0 fusion.6
  169.2 2.7 fusion.5
  171.9 186.7 %all-gather.6.cloned.1.call-done = bf16[128,4,2880]{2,1,0:T(4,128)(2,1)} async-done(((bf16[1,4,2880]{2,1,0:T(4,128)(2,1)}), bf16[128,4,2880]{2,1,0:T(4,128)(2,1)}) %all-gather.6.cloned.1.call-update) | async-done | bytes 2949136 | tf_op jit(solution)/shard_map/all_gather | solution.py:122
  358.6 4.4 %reshape.171 = bf16[512,2880]{1,0:T(8,128)(2,1)S(1)} reshape(bf16[128,4,2880]{2,1,0:T(4,128)(2,1)} %all-gather.6.cloned.1.call-done) | data formatting | bytes 5898240
  363.0 1.6 gather_fusion.1
  (54 shorter events, 10.0 us)
Async XLA Ops:
  8.1 10.2 %collective-permute-start.1 = (bf16[1,320,128]{2,1,0:T(8,128)(2,1)S(1)}, bf16[1,320,128]{2,1,0:T(8,128)(2,1)S(1)}, u32[]{:S(2)}, u32[]{:S(2)}) collective-permute-start(bf16[1,320,128]{2,1,0:T(8,128)(2,1)S(1)} %fusion.17), channel_id=1, source_target_pairs={{1,0},{2,1},{3,2},{5,4},{6,5},{7,6},{9,8},{10,9},{11,10},{13,12},{... | collective-permute-start | bytes 245768 | tf_op jit(solution)/shard_map/ppermute | solution.py:24
  9.4 8.9 %collective-permute-start = (bf16[1,320,128]{2,1,0:T(8,128)(2,1)S(1)}, bf16[1,320,128]{2,1,0:T(8,128)(2,1)S(1)}, u32[]{:S(2)}, u32[]{:S(2)}) collective-permute-start(bf16[1,320,128]{2,1,0:T(8,128)(2,1)S(1)} %fusion.17), channel_id=1, source_target_pairs={{0,1},{1,2},{2,3},{4,5},{5,6},{6,7},{8,9},{9,10},{10,11},{12,13},{... | collective-permute-start | bytes 245768 | tf_op jit(solution)/shard_map/ppermute | solution.py:22
  20.0 0.9 copy-start.1
  34.4 83.7 %all-to-all-start = ((bf16[128,4,2880]{2,1,0:T(4,128)(2,1)}), bf16[128,4,2880]{2,1,0:T(4,128)(2,1)S(1)}, u32[]{:S(2)}, u32[]{:S(2)}) async-start(bf16[128,4,2880]{2,1,0:T(4,128)(2,1)} %select_convert_fusion), calls=%async_computation | async-start | bytes 6029312 | tf_op jit(solution)/shard_map/all_to_all | solution.py:109
  47.9 96.6 %copy-start.5 = (f32[4,2880]{1,0:T(4,128)S(1)}, f32[4,2880]{1,0:T(4,128)}, u32[]{:S(2)}) copy-start(f32[4,2880]{1,0:T(4,128)} %param.10) | copy-start | bytes 138244
  48.0 96.6 %copy-start.6 = (f32[4,2880]{1,0:T(4,128)S(1)}, f32[4,2880]{1,0:T(4,128)}, u32[]{:S(2)}) copy-start(f32[4,2880]{1,0:T(4,128)} %param.12) | copy-start | bytes 138244
  48.0 96.6 %copy-start.7 = (f32[4,2880]{1,0:T(4,128)S(1)}, f32[4,2880]{1,0:T(4,128)}, u32[]{:S(2)}) copy-start(f32[4,2880]{1,0:T(4,128)} %param.11) | copy-start | bytes 138244
  48.0 97.3 %copy-start.3 = (bf16[1,1,320,128]{3,2,1,0:T(8,128)(2,1)S(1)}, bf16[1,1,320,128]{3,2,1,0:T(8,128)(2,1)}, u32[]{:S(2)}) copy-start(bf16[1,1,320,128]{3,2,1,0:T(8,128)(2,1)} %param.8) | copy-start | bytes 245764
  48.0 112.4 %all-gather.4.cloned.1.call-start = ((), (), s32[]{:S(2)}) async-start(), calls=%async_computation.1 | async-start | bytes 2355200 | tf_op jit(solution)/shard_map/all_gather | solution.py:74
  48.7 309.9 %all-gather.6.cloned.1.call-start = ((), (), s32[]{:S(2)}) async-start(), calls=%async_computation.2 | async-start | bytes 3038208 | tf_op jit(solution)/shard_map/all_gather | solution.py:122
  145.3 7.2 %collective-permute-start.3 = (bf16[1,320,128]{2,1,0:T(8,128)(2,1)S(1)}, bf16[1,320,128]{2,1,0:T(8,128)(2,1)S(1)}, u32[]{:S(2)}, u32[]{:S(2)}) collective-permute-start(bf16[1,320,128]{2,1,0:T(8,128)(2,1)S(1)} %bitcast.61), channel_id=1, source_target_pairs={{1,0},{2,1},{3,2},{5,4},{6,5},{7,6},{9,8},{10,9},{11,10},{13,12},{... | collective-permute-start | bytes 245768 | tf_op jit(solution)/shard_map/ppermute | solution.py:24
  146.6 7.5 %collective-permute-start.2 = (bf16[1,320,128]{2,1,0:T(8,128)(2,1)S(1)}, bf16[1,320,128]{2,1,0:T(8,128)(2,1)S(1)}, u32[]{:S(2)}, u32[]{:S(2)}) collective-permute-start(bf16[1,320,128]{2,1,0:T(8,128)(2,1)S(1)} %bitcast.62), channel_id=1, source_target_pairs={{0,1},{1,2},{2,3},{4,5},{5,6},{6,7},{8,9},{9,10},{10,11},{12,13},{... | collective-permute-start | bytes 245768 | tf_op jit(solution)/shard_map/ppermute | solution.py:22
  163.7 2.5 copy-start.2
  163.7 2.5 copy-start.4
  166.2 3.0 copy-start
Sparse Core Ops, SparseCore 0:
  50.9 76.2 all-gather.3
  145.4 213.1 all-gather.5
where the time goes:
time: 372 us; the launch traced here: 371 us
  waiting for transfers between devices  258 us (69%)
  starting transfers between devices  28.5 us (8%)
  local copies, waits for them, and re-layouts  27.6 us (7%)
  blocking collectives  25.1 us (7%)
  between operations  14.3 us (4%)
  other arithmetic  10.2 us (3%)
  matrix products  7.22 us (2%)
    all_gather x1, waiting for transfers between devices, local(): lax.all_gather(new_master.astype(jnp.bfloat16), 'dp', axis=0, tiled=True)  187 us
    all_to_all x1, waiting for transfers between devices, local(): lax.all_to_all(outgoing.astype(jnp.bfloat16), 'dp', split_axis=0, concat_...  69.2 us
    psum x1, blocking collectives, local(): lax.psum(jnp.sum(incoming, axis=0).astype(jnp.bfloat16), 'strip')  25.1 us
    all_to_all x1, starting transfers between devices, local(): lax.all_to_all(outgoing.astype(jnp.bfloat16), 'dp', split_axis=0, concat_...  13.5 us
    ppermute x2, starting transfers between devices, extended(): lax.ppermute(tail, axis, [(i, (i + 1) % count) for i in range(ends)])  12.3 us
    unnamed x32, local copies, waits for them, and re-layouts  10.9 us
    gather x2, local copies, waits for them, and re-layouts, local(): jnp.take(partial_grad, source_row, axis=0, mode='fill', fill_value=0.0)  8.37 us
  transfers between devices with their start and end apart: 7, of which 4 were waited for; matrix products, arithmetic and copies ran while one was open for 6% of the time, Pallas kernels for 0%

commit v1 on v0

--- a/solution.py
+++ b/solution.py
@@ -119,7 +119,9 @@
     new_master, new_first, new_second = adam_update(
         gradient, master, first_moment, second_moment, my_filled
     )
-    published = lax.all_gather(new_master.astype(jnp.bfloat16), "dp", axis=0, tiled=True)
+    part = new_master.astype(jnp.bfloat16)
+    repeated = jnp.stack([part] * lax.axis_size("dp"))
+    published = jnp.concatenate(lax.all_to_all(repeated, "dp", 0, 0), axis=0)
     quarter = weight.shape[0]
     wanted = lax.dynamic_slice_in_dim(slot_ids, lax.axis_index("strip") * quarter, quarter)
     new_weight = published[wanted]

time: 372 us -> 255 us (0.69)
  the two profiles are of different devices: /device:TPU:8 before, /device:TPU:1 now
where the time goes in v1:
time: 255 us; the launch traced here: 254 us
  waiting for transfers between devices  129 us (51%)
  starting transfers between devices  42.1 us (17%)
  local copies, waits for them, and re-layouts  30.1 us (12%)
  blocking collectives  20.8 us (8%)
  between operations  14.3 us (6%)
  other arithmetic  10.2 us (4%)
  matrix products  7.21 us (3%)
    all_to_all x1, waiting for transfers between devices, local(): lax.all_to_all(outgoing.astype(jnp.bfloat16), 'dp', split_axis=0, concat_...  69.1 us
    all_gather x1, waiting for transfers between devices, local(): full_weight = lax.all_gather(weight, 'strip', axis=0, tiled=True)  57.6 us
    psum x1, blocking collectives, local(): lax.psum(jnp.sum(incoming, axis=0).astype(jnp.bfloat16), 'strip')  20.8 us
    all_to_all x1, starting transfers between devices, local(): lax.all_to_all(outgoing.astype(jnp.bfloat16), 'dp', split_axis=0, concat_...  14 us
    all_to_all x1, starting transfers between devices, local(): published = jnp.concatenate(lax.all_to_all(repeated, 'dp', 0, 0), axis=0)  13.3 us
    ppermute x2, starting transfers between devices, extended(): lax.ppermute(tail, axis, [(i, (i + 1) % count) for i in range(ends)])  12.1 us
    gather x2, local copies, waits for them, and re-layouts, local(): jnp.take(partial_grad, source_row, axis=0, mode='fill', fill_value=0.0)  8.37 us
    unnamed x31, local copies, waits for them, and re-layouts  6.55 us
  transfers between devices with their start and end apart: 7, of which 4 were waited for; matrix products, arithmetic and copies ran while one was open for 8% of the time, Pallas kernels for 0%

profile of v1, /device:TPU:1, one launch (start us, length us, event | category | flops | bytes accessed | tf_op | source)
XLA Modules:
  0.0 253.7 jit_solution(17353990538246742195)
XLA Ops:
  8.1 1.3 collective-permute-start.1
  9.4 7.3 %collective-permute-start = (bf16[1,320,128]{2,1,0:T(8,128)(2,1)S(1)}, bf16[1,320,128]{2,1,0:T(8,128)(2,1)S(1)}, u32[]{:S(2)}, u32[]{:S(2)}) collective-permute-start(bf16[1,320,128]{2,1,0:T(8,128)(2,1)S(1)} %fusion.17), channel_id=1, source_target_pairs={{0,1},{1,2},{2,3},{4,5},{5,6},{6,7},{8,9},{9,10},{10,11},{12,13},{... | collective-permute-start | bytes 245768 | tf_op jit(solution)/shard_map/ppermute | solution.py:22
  16.7 1.0 convert_reduce_fusion
  19.3 1.0 constant_dynamic-update-slice_fusion.1
  21.4 1.5 convolution_bitcast_fusion
  22.9 3.7 %gather_fusion = bf16[512,2880]{1,0:T(8,128)(2,1)} fusion(bf16[320,2880]{1,0:T(8,128)(2,1)S(1)} %convolution_bitcast_fusion, s32[1024]{0:T(1024)S(1)} %pad_clamp_fusion.1), kind=kCustom, calls=%fused_computation | custom fusion | bytes 5900288 | tf_op jit(solution)/shard_map/jit(_take)/gather | solution.py:106
  26.6 4.7 %gather.10 = bf16[128,4,2880]{2,1,0:T(4,128)(2,1)S(1)} reshape(bf16[512,2880]{1,0:T(8,128)(2,1)} %gather_fusion) | data formatting | bytes 5898240 | tf_op jit(solution)/shard_map/jit(_take)/gather | solution.py:106
  31.3 3.7 %select_convert_fusion = bf16[128,4,2880]{2,1,0:T(4,128)(2,1)} fusion(bf16[128,4,2880]{2,1,0:T(4,128)(2,1)S(1)} %gather.10, pred[128,4]{1,0:T(8,128)(4,1)S(1)} %compare_and_fusion), kind=kLoop, calls=%fused_computation.2 | loop fusion | flops 1474560 | bytes 5898752 | tf_op jit(solution)/shard_map/convert_element_type | solution.py:110
  35.0 14.0 %all-to-all-start = ((bf16[128,4,2880]{2,1,0:T(4,128)(2,1)}), bf16[128,4,2880]{2,1,0:T(4,128)(2,1)S(1)}, u32[]{:S(2)}, u32[]{:S(2)}) async-start(bf16[128,4,2880]{2,1,0:T(4,128)(2,1)} %select_convert_fusion), calls=%async_computation | async-start | bytes 6029312 | tf_op jit(solution)/shard_map/all_to_all | solution.py:109
  49.1 69.1 %all-to-all-done = bf16[128,4,2880]{2,1,0:T(4,128)(2,1)S(1)} async-done(((bf16[128,4,2880]{2,1,0:T(4,128)(2,1)}), bf16[128,4,2880]{2,1,0:T(4,128)(2,1)S(1)}, u32[]{:S(2)}, u32[]{:S(2)}) %all-to-all-start) | async-done | bytes 2949152 | tf_op jit(solution)/shard_map/all_to_all | solution.py:109
  118.2 1.3 reduce_sum.32
  119.5 20.8 %psum.7 = bf16[4,2880]{1,0:T(4,128)(2,1)S(1)} all-reduce(bf16[4,2880]{1,0:T(4,128)(2,1)S(1)} %reduce_sum.32), channel_id=1, replica_groups=mesh['dp'=128,'strip'=4] {'strip'}, use_global_device_ids=true, to_apply=%region_4.5 | all-reduce | flops 11520 | bytes 46080 | tf_op jit(solution)/shard_map/psum | solution.py:112
  141.0 2.4 stack.2
  143.5 13.3 %all-to-all-start.1 = ((bf16[128,4,2880]{2,1,0:T(4,128)(2,1)}), bf16[128,4,2880]{2,1,0:T(4,128)(2,1)}, u32[]{:S(2)}, u32[]{:S(2)}) async-start(bf16[128,4,2880]{2,1,0:T(4,128)(2,1)} %stack.2), calls=%async_computation.1 | async-start | bytes 6029312 | tf_op jit(solution)/shard_map/all_to_all | solution.py:124
  157.5 1.3 collective-permute-start.3
  158.8 4.9 %collective-permute-start.2 = (bf16[1,320,128]{2,1,0:T(8,128)(2,1)S(1)}, bf16[1,320,128]{2,1,0:T(8,128)(2,1)S(1)}, u32[]{:S(2)}, u32[]{:S(2)}) collective-permute-start(bf16[1,320,128]{2,1,0:T(8,128)(2,1)S(1)} %bitcast.60), channel_id=1, source_target_pairs={{0,1},{1,2},{2,3},{4,5},{5,6},{6,7},{8,9},{9,10},{10,11},{12,13},{... | collective-permute-start | bytes 245768 | tf_op jit(solution)/shard_map/ppermute | solution.py:22
  164.4 1.1 collective-permute-done.2
  171.7 57.6 %all-gather.2.cloned.1.call-done = bf16[320,2880]{1,0:T(8,128)(2,1)} async-done(((bf16[80,2880]{1,0:T(8,128)(2,1)}), bf16[320,2880]{1,0:T(8,128)(2,1)}) %all-gather.2.cloned.1.call-update) | async-done | bytes 1843216 | tf_op jit(solution)/shard_map/all_gather | solution.py:74
  229.3 3.3 %copy.17 = bf16[320,2880]{0,1:T(8,128)(2,1)S(1)} copy(bf16[320,2880]{1,0:T(8,128)(2,1)} %all-gather.2.cloned.1.call-done) | data formatting | bytes 3686400 | tf_op jit(solution)/shard_map/all_gather | solution.py:74
  232.6 2.5 copy.18
  235.2 3.0 %fusion.6 = bf16[1,1,320,128]{3,2,1,0:T(8,128)(2,1)} fusion(bf16[320,2880]{1,0:T(8,128)(2,1)} %all-gather.2.cloned.1.call-done, bf16[1,2880,128]{2,1,0:T(8,128)(2,1)S(1)} %copy-done.2, bf16[1,1,320,128]{3,2,1,0:T(8,128)(2,1)S(1)} %copy-done.4), kind=kOutput, calls=%fused_computation.14 | convolution fusion | flops 236052480 | bytes 2744320 | tf_op jit(solution)/shard_map/ok,hkw->how/dot_general | solution.py:82
  238.1 2.7 %fusion.5 = bf16[1,1,320,128]{3,2,1,0:T(8,128)(2,1)} fusion(bf16[320,2880]{0,1:T(8,128)(2,1)S(1)} %bitcast.58, bf16[1,2880,128]{2,1,0:T(8,128)(2,1)} %slice_dynamic-update-slice_fusion, bf16[1,1,320,128]{3,2,1,0:T(8,128)(2,1)S(1)} %copy-done.4, bf16[1,1,320,128]{3,2,1,0:T(8,128)(2,1)S(1)} %copy-done.3), kind=kOutput, calls=%fused_computation.13 | convolution fusion | flops 236421120 | bytes 2826240 | tf_op jit(solution)/shard_map/ck,hkw->hcw/dot_general | solution.py:88
  240.8 4.4 %reshape.157 = bf16[512,2880]{1,0:T(8,128)(2,1)S(1)} reshape(bf16[128,4,2880]{2,1,0:T(4,128)(2,1)} %all-to-all-done.1) | data formatting | bytes 5898240 | tf_op jit(solution)/shard_map/reshape | solution.py:124
  245.2 1.6 gather_fusion.1
  (54 shorter events, 12.1 us)
Async XLA Ops:
  8.1 10.7 %collective-permute-start.1 = (bf16[1,320,128]{2,1,0:T(8,128)(2,1)S(1)}, bf16[1,320,128]{2,1,0:T(8,128)(2,1)S(1)}, u32[]{:S(2)}, u32[]{:S(2)}) collective-permute-start(bf16[1,320,128]{2,1,0:T(8,128)(2,1)S(1)} %fusion.17), channel_id=1, source_target_pairs={{1,0},{2,1},{3,2},{5,4},{6,5},{7,6},{9,8},{10,9},{11,10},{13,12},{... | collective-permute-start | bytes 245768 | tf_op jit(solution)/shard_map/ppermute | solution.py:24
  9.4 9.4 %collective-permute-start = (bf16[1,320,128]{2,1,0:T(8,128)(2,1)S(1)}, bf16[1,320,128]{2,1,0:T(8,128)(2,1)S(1)}, u32[]{:S(2)}, u32[]{:S(2)}) collective-permute-start(bf16[1,320,128]{2,1,0:T(8,128)(2,1)S(1)} %fusion.17), channel_id=1, source_target_pairs={{0,1},{1,2},{2,3},{4,5},{5,6},{6,7},{8,9},{9,10},{10,11},{12,13},{... | collective-permute-start | bytes 245768 | tf_op jit(solution)/shard_map/ppermute | solution.py:22
  20.5 0.9 copy-start.1
  35.0 83.2 %all-to-all-start = ((bf16[128,4,2880]{2,1,0:T(4,128)(2,1)}), bf16[128,4,2880]{2,1,0:T(4,128)(2,1)S(1)}, u32[]{:S(2)}, u32[]{:S(2)}) async-start(bf16[128,4,2880]{2,1,0:T(4,128)(2,1)} %select_convert_fusion), calls=%async_computation | async-start | bytes 6029312 | tf_op jit(solution)/shard_map/all_to_all | solution.py:109
  49.0 91.2 %copy-start.5 = (f32[4,2880]{1,0:T(4,128)S(1)}, f32[4,2880]{1,0:T(4,128)}, u32[]{:S(2)}) copy-start(f32[4,2880]{1,0:T(4,128)} %param.10) | copy-start | bytes 138244
  49.0 91.2 %copy-start.6 = (f32[4,2880]{1,0:T(4,128)S(1)}, f32[4,2880]{1,0:T(4,128)}, u32[]{:S(2)}) copy-start(f32[4,2880]{1,0:T(4,128)} %param.12) | copy-start | bytes 138244
  49.0 91.2 %copy-start.7 = (f32[4,2880]{1,0:T(4,128)S(1)}, f32[4,2880]{1,0:T(4,128)}, u32[]{:S(2)}) copy-start(f32[4,2880]{1,0:T(4,128)} %param.11) | copy-start | bytes 138244
  143.5 14.0 %copy-start.3 = (bf16[1,1,320,128]{3,2,1,0:T(8,128)(2,1)S(1)}, bf16[1,1,320,128]{3,2,1,0:T(8,128)(2,1)}, u32[]{:S(2)}) copy-start(bf16[1,1,320,128]{3,2,1,0:T(8,128)(2,1)} %param.8) | copy-start | bytes 245764
  143.5 97.4 %all-to-all-start.1 = ((bf16[128,4,2880]{2,1,0:T(4,128)(2,1)}), bf16[128,4,2880]{2,1,0:T(4,128)(2,1)}, u32[]{:S(2)}, u32[]{:S(2)}) async-start(bf16[128,4,2880]{2,1,0:T(4,128)(2,1)} %stack.2), calls=%async_computation.1 | async-start | bytes 6029312 | tf_op jit(solution)/shard_map/all_to_all | solution.py:124
  156.8 72.5 %all-gather.2.cloned.1.call-start = ((), (), s32[]{:S(2)}) async-start(), calls=%async_computation.2 | async-start | bytes 2355200 | tf_op jit(solution)/shard_map/all_gather | solution.py:74
  157.5 6.9 %collective-permute-start.3 = (bf16[1,320,128]{2,1,0:T(8,128)(2,1)S(1)}, bf16[1,320,128]{2,1,0:T(8,128)(2,1)S(1)}, u32[]{:S(2)}, u32[]{:S(2)}) collective-permute-start(bf16[1,320,128]{2,1,0:T(8,128)(2,1)S(1)} %bitcast.59), channel_id=1, source_target_pairs={{1,0},{2,1},{3,2},{5,4},{6,5},{7,6},{9,8},{10,9},{11,10},{13,12},{... | collective-permute-start | bytes 245768 | tf_op jit(solution)/shard_map/ppermute | solution.py:24
  158.8 6.7 %collective-permute-start.2 = (bf16[1,320,128]{2,1,0:T(8,128)(2,1)S(1)}, bf16[1,320,128]{2,1,0:T(8,128)(2,1)S(1)}, u32[]{:S(2)}, u32[]{:S(2)}) collective-permute-start(bf16[1,320,128]{2,1,0:T(8,128)(2,1)S(1)} %bitcast.60), channel_id=1, source_target_pairs={{0,1},{1,2},{2,3},{4,5},{5,6},{6,7},{8,9},{9,10},{10,11},{12,13},{... | collective-permute-start | bytes 245768 | tf_op jit(solution)/shard_map/ppermute | solution.py:22
  232.6 2.5 %copy-start.2 = (bf16[1,2880,128]{2,1,0:T(8,128)(2,1)S(1)}, bf16[1,2880,128]{2,1,0:T(8,128)(2,1)}, u32[]{:S(2)}) copy-start(bf16[1,2880,128]{2,1,0:T(8,128)(2,1)} %copy-done.1) | copy-start | bytes 2211844
  232.6 2.5 copy-start.4
  235.2 3.0 %copy-start = (bf16[320,9,320]{0,2,1:T(8,128)(2,1)S(1)}, bf16[320,9,320]{0,2,1:T(8,128)(2,1)}, u32[]{:S(2)}) copy-start(bf16[320,9,320]{0,2,1:T(8,128)(2,1)} %copy.18) | copy-start | bytes 5529604
Sparse Core Ops, SparseCore 0:
  159.7 69.5 all-gather.1
